TPU v7x, 32 devices: a whole 2x2x4 slice. The times are simulated.
32 devices in a mesh: dp: 4 (over z), ctx: 2 (over core), tp: 4 (over y, x).
Axes of the slice: x: 2, y: 2, z: 4, core: 2. Of those that a mesh axis runs over, the one named last changes fastest.
Arguments:
- block_in: bfloat16 [8192, 2048], P(('dp', 'ctx')), may hold values from -6 to 6
- query_proj: bfloat16 [2048, 2048], P('dp', 'tp'), may hold values from -0.125 to 0.125
- forget_proj: bfloat16 [2048, 2048], P('dp', 'tp'), may hold values from -0.0625 to 0.0625
- value_proj: bfloat16 [2048, 2048], P('dp', 'tp'), may hold values from -0.125 to 0.125
- outgate_proj: bfloat16 [2048, 2048], P('dp', 'tp'), may hold values from -0.125 to 0.125
- out_proj: bfloat16 [2048, 2048], P('tp', 'dp'), may hold values from -0.125 to 0.125
- ffn_gate: bfloat16 [2048, 5632], P('dp', 'tp'), may hold values from -0.125 to 0.125
- ffn_up: bfloat16 [2048, 5632], P('dp', 'tp'), may hold values from -0.125 to 0.125
- ffn_down: bfloat16 [5632, 2048], P('tp', 'dp'), may hold values from -0.078125 to 0.078125
- first_gain: float32 [2048], replicated, may hold values from 0.5 to 1.5
- second_gain: float32 [2048], replicated, may hold values from 0.5 to 1.5
- group_gain: float32 [2048], P('tp'), may hold values from 0.5 to 1.5
- forget_bias: float32 [2048], P('tp'), may hold values from 3 to 12
- bound_table: float32 [24, 2048], P(None, 'tp'), may hold values from -4 to 4
- layer_index: int32 [1], replicated, may hold values from 1 to 23
- second_start: int32 [4], P('dp'), may hold values from 1 to 2048, as said below
- cotangent: bfloat16 [8192, 2048], P(('dp', 'ctx')), may hold values from -6 to 6
Outputs:
- block_out: bfloat16 [8192, 2048], P(('dp', 'ctx'))
- input_grad: float32 [8192, 2048], P(('dp', 'ctx'))
- query_grad: float32 [2048, 2048], P('dp', 'tp')
- forget_grad: float32 [2048, 2048], P('dp', 'tp')
- value_grad: float32 [2048, 2048], P('dp', 'tp')
- outgate_grad: float32 [2048, 2048], P('dp', 'tp')
- out_proj_grad: float32 [2048, 2048], P('tp', 'dp')
- ffn_gate_grad: float32 [2048, 5632], P('dp', 'tp')
- ffn_up_grad: float32 [2048, 5632], P('dp', 'tp')
- ffn_down_grad: float32 [5632, 2048], P('tp', 'dp')
- first_gain_grad: float32 [2048], replicated
- second_gain_grad: float32 [2048], replicated
- group_gain_grad: float32 [2048], P('tp')
- forget_bias_grad: float32 [2048], P('tp')
- bound_table_grad: float32 [24, 2048], P(None, 'tp')
Inputs may be any that keep to these rules, and one draw needn't show every extreme that they name: second_start[p] is 2048 where pack p is one whole sequence, and otherwise the position inside the pack where its second sequence begins; pack 0 is always one whole sequence and pack 1 always holds two. layer_index names a row of bound_table other than the first.
All inputs are finite; a program needn't handle non-finite values.
Results may differ from a plain program's by a relative error of at most 0.018.
Values may be sent and summed in bfloat16 or wider, within the bound.
No kernel may reach another device: no remote copies, remote signals or barrier semaphores. Data moves between devices by JAX's collectives and lax.ppermute only.
A program may use at most 384 MiB of HBM per device.

v0:
```python
import jax
import jax.numpy as jnp
from jax import lax
from jax.sharding import PartitionSpec as P

HEAD = 128
BLOCK = 32
HIGH = lax.Precision.HIGHEST
EPS_NORM = 1e-06
EPS_GROUP = 1e-05


def carried_in(value, axis, join, neutral):
    count, mine = (lax.axis_size(axis), lax.axis_index(axis))
    pieces = jax.tree.map(lambda part: lax.all_gather(part, axis), value)
    total = jax.tree.map(
        lambda part, zero: jnp.full_like(part, 0) + jnp.asarray(zero, part.dtype), value, neutral
    )

    def hop(position, total):
        longer = join(total, jax.tree.map(lambda part: part[position], pieces))
        return jax.tree.map(lambda new, old: jnp.where(position < mine, new, old), longer, total)

    return lax.fori_loop(0, count - 1, hop, total)


def carried_in_2(array, axis, combine, identity):
    peers, index = (lax.axis_size(axis), lax.axis_index(axis))
    everything = jax.tree.map(
        lambda part, kind: lax.all_gather(part.astype(kind), axis),
        array,
        jax.tree.map(lambda a: jnp.bfloat16 if a.dtype == jnp.float32 else a.dtype, array),
    )
    start = jax.tree.map(
        lambda part, zero: jnp.broadcast_to(jnp.asarray(zero, part.dtype), part.shape),
        array,
        identity,
    )

    def hop(k, before):
        at = peers - 1 - k
        reached = at > index
        new = combine(
            before, jax.tree.map(lambda part, own: part[at].astype(own.dtype), everything, array)
        )
        return jax.tree.map(lambda a, b: jnp.where(reached, a, b), new, before)

    return lax.fori_loop(0, peers, hop, start)


def rms_norm(rows_in, gain_vec):
    return (
        rows_in
        * lax.rsqrt(jnp.mean(rows_in * rows_in, axis=-1, keepdims=True) + EPS_NORM)
        * gain_vec
    )


def head_norm(mixed, pre_gate, gain_vec, head_count):
    row_count = mixed.shape[0]
    grouped = mixed.reshape(row_count, head_count, -1)
    scaled = grouped * lax.rsqrt(jnp.mean(grouped * grouped, axis=-1, keepdims=True) + EPS_GROUP)
    return scaled.reshape(row_count, -1) * gain_vec * jax.nn.silu(pre_gate)


def lower_bound(bound_rows, which_layer):
    weights = jax.nn.softmax(bound_rows, axis=0)
    rising = jnp.cumsum(weights, axis=0) - weights[0:1]
    picked = (
        lax.broadcasted_iota(jnp.int32, (bound_rows.shape[0], 1), 0) == which_layer[0]
    ).astype(bound_rows.dtype)
    return jnp.sum(rising * picked, axis=0)


def gate_values(pre_query, pre_forget, bias_vec, bound_vec):
    shifted = pre_forget + bias_vec
    forget = bound_vec + (1.0 - bound_vec) * jax.nn.sigmoid(shifted)
    return (jax.nn.silu(pre_query), (1.0 - bound_vec) * jax.nn.sigmoid(-shifted), jnp.log(forget))


def chain_link(earlier, later):
    return (earlier[0] * later[0], later[0][..., None] * earlier[1] + later[1])


def contract_last(left_side, right_side):
    return lax.dot_general(
        left_side, right_side, (((1,), (1,)), ((), ())), preferred_element_type=jnp.float32
    )


def contract_first(left_side, right_side):
    return lax.dot_general(
        left_side, right_side, (((0,), (0,)), ((), ())), preferred_element_type=jnp.float32
    )


def block_parts(queries, key_rows, values, log_forget, doc_ids, prev_doc, block_len):
    length, head_count, feature = queries.shape
    block_count = length // block_len
    blocked = (block_count, block_len, head_count, feature)
    queries = queries.reshape(blocked)
    key_rows = key_rows.reshape(blocked)
    values = values.reshape(blocked)
    decays = jnp.cumsum(log_forget.reshape(blocked), axis=1)
    doc_ids = doc_ids.reshape(block_count, block_len)
    before = jnp.concatenate([jnp.reshape(prev_doc, (1,)), doc_ids[:-1, block_len - 1]])
    middle = decays[:, block_len // 2 : block_len // 2 + 1]
    final_decay = decays[:, block_len - 1 :]
    scores = jnp.einsum(
        "nthc,nshc->nhts",
        queries * jnp.exp(decays - middle),
        key_rows * jnp.exp(middle - decays),
        precision=HIGH,
    )
    causal = lax.broadcasted_iota(jnp.int32, (block_len, block_len), 0) >= lax.broadcasted_iota(
        jnp.int32, (block_len, block_len), 1
    )
    allowed = causal[None] & (doc_ids[:, :, None] == doc_ids[:, None, :])
    scores = jnp.where(allowed[:, None], scores, 0.0)
    inside = jnp.einsum("nhts,nshe->nthe", scores, values, precision=HIGH)
    in_tail = (doc_ids == doc_ids[:, block_len - 1 :]).astype(decays.dtype)
    ending = key_rows * jnp.exp(final_decay - decays) * in_tail[:, :, None, None]
    states = jnp.einsum("nshc,nshe->nhce", ending, values, precision=HIGH)
    kept_flag = (doc_ids[:, block_len - 1] == before).astype(decays.dtype)
    carried = jnp.exp(final_decay[:, 0]) * kept_flag[:, None, None]
    entering = (doc_ids == before[:, None]).astype(decays.dtype)
    reached = queries * jnp.exp(decays) * entering[:, :, None, None]
    prefix_decay, prefix_state = lax.associative_scan(chain_link, (carried, states), axis=0)
    return (inside, reached, prefix_decay, prefix_state)


def finish(pieces, state_in):
    inside, reached, prefix_decay, prefix_state = pieces
    state_ends = prefix_decay[..., None] * state_in[None] + prefix_state
    state_starts = jnp.concatenate([state_in[None], state_ends[:-1]], axis=0)
    outside = jnp.einsum("nthc,nhce->nthe", reached, state_starts, precision=HIGH)
    summed = inside + outside
    block_count, block_len, head_count, feature = summed.shape
    return (summed.reshape(block_count * block_len, head_count, feature), state_ends[-1])


def body(
    block_in,
    query_proj,
    forget_proj,
    value_proj,
    outgate_proj,
    out_proj,
    ffn_gate,
    ffn_up,
    ffn_down,
    first_gain,
    second_gain,
    group_gain,
    forget_bias,
    bound_table,
    layer_index,
    second_start,
    cotangent,
):
    row_count = block_in.shape[0]
    local_width = query_proj.shape[1]
    head_count = local_width // HEAD
    hidden_width = ffn_gate.shape[1]
    inputs = block_in.astype(jnp.float32)
    first_low = rms_norm(inputs, first_gain).astype(jnp.bfloat16)
    mix_local = jnp.concatenate([query_proj, forget_proj, value_proj, outgate_proj], axis=1)
    ffn_local = jnp.concatenate([ffn_gate, ffn_up], axis=1)
    mix_full, out_full = (
        lax.all_gather(mix_local, "dp", axis=0, tiled=True),
        lax.all_gather(out_proj, "dp", axis=1, tiled=True),
    )
    projected = jnp.dot(first_low, mix_full, preferred_element_type=jnp.float32)
    pre_query = projected[:, :local_width]
    pre_forget = projected[:, local_width : 2 * local_width]
    pre_value = projected[:, 2 * local_width : 3 * local_width]
    pre_outgate = projected[:, 3 * local_width :]
    bound_vec = lower_bound(bound_table, layer_index)
    queries, key_rows, log_forget = gate_values(pre_query, pre_forget, forget_bias, bound_vec)
    offset = lax.axis_index("ctx") * row_count
    doc_ids = (offset + lax.iota(jnp.int32, row_count) >= second_start[0]).astype(jnp.int32)
    prev_doc = (offset - 1 >= second_start[0]).astype(jnp.int32)

    def to_heads(flat):
        return flat.reshape(row_count, head_count, HEAD)

    def mixer(queries_in, keys_in, values_in, logs_in, state_in):
        return finish(
            block_parts(queries_in, keys_in, values_in, logs_in, doc_ids, prev_doc, BLOCK), state_in
        )

    pieces = block_parts(
        to_heads(queries),
        to_heads(key_rows),
        to_heads(pre_value),
        to_heads(log_forget),
        doc_ids,
        prev_doc,
        BLOCK,
    )
    identity = (
        jnp.ones((head_count, HEAD), jnp.float32),
        jnp.zeros((head_count, HEAD, HEAD), jnp.float32),
    )
    shard_decay = pieces[2][-1]
    entry_pair = carried_in((shard_decay, pieces[3][-1]), "ctx", chain_link, identity)
    state_in = entry_pair[1]
    mixed, _ = finish(pieces, state_in)
    mixed_flat = mixed.reshape(row_count, local_width)
    gated_low = head_norm(mixed_flat, pre_outgate, group_gain, head_count).astype(jnp.bfloat16)
    mix_partial = jnp.dot(gated_low, out_full, preferred_element_type=jnp.float32)
    resid = inputs + lax.psum(mix_partial, "tp")
    second_low = rms_norm(resid, second_gain).astype(jnp.bfloat16)
    ffn_full, down_full = (
        lax.all_gather(ffn_local, "dp", axis=0, tiled=True),
        lax.all_gather(ffn_down, "dp", axis=1, tiled=True),
    )
    gate_up = jnp.dot(second_low, ffn_full, preferred_element_type=jnp.float32)
    pre_gate = gate_up[:, :hidden_width]
    pre_up = gate_up[:, hidden_width:]
    hidden_low = (jax.nn.silu(pre_gate) * pre_up).astype(jnp.bfloat16)
    ffn_partial = jnp.dot(hidden_low, down_full, preferred_element_type=jnp.float32)
    block_out = (
        resid + lax.psum(ffn_partial.astype(jnp.bfloat16), "tp").astype(jnp.float32)
    ).astype(jnp.bfloat16)
    mix_full, out_full, ffn_full, down_full = (
        lax.all_gather(mix_local, "dp", axis=0, tiled=True),
        lax.all_gather(out_proj, "dp", axis=1, tiled=True),
        lax.all_gather(ffn_local, "dp", axis=0, tiled=True),
        lax.all_gather(ffn_down, "dp", axis=1, tiled=True),
    )
    cotangent_full = cotangent.astype(jnp.float32)
    hidden_grad = contract_last(cotangent, down_full)
    down_weight_grad = contract_first(hidden_low, cotangent)
    _, act_pull = jax.vjp(lambda gate_in, up_in: jax.nn.silu(gate_in) * up_in, pre_gate, pre_up)
    gate_grad, up_grad = act_pull(hidden_grad)
    gate_up_grad = jnp.concatenate([gate_grad, up_grad], axis=1).astype(jnp.bfloat16)
    second_part = contract_last(gate_up_grad, ffn_full)
    ffn_weight_grad = contract_first(second_low, gate_up_grad)
    second_total = lax.psum(second_part, "tp")
    _, second_pull = jax.vjp(rms_norm, resid, second_gain)
    resid_part, second_gain_grad = second_pull(second_total)
    resid_grad = cotangent_full + resid_part
    resid_low = resid_grad.astype(jnp.bfloat16)
    gated_grad = contract_last(resid_low, out_full)
    out_weight_grad = contract_first(gated_low, resid_low)
    _, head_pull = jax.vjp(
        lambda mixed_in, gate_in, gain_in: head_norm(mixed_in, gate_in, gain_in, head_count),
        mixed_flat,
        pre_outgate,
        group_gain,
    )
    mixed_grad, outgate_pre_grad, group_gain_grad = head_pull(gated_grad)
    _, mixer_pull = jax.vjp(
        mixer,
        to_heads(queries),
        to_heads(key_rows),
        to_heads(pre_value),
        to_heads(log_forget),
        state_in,
    )
    first_pass = mixer_pull(
        (to_heads(mixed_grad), jnp.zeros((head_count, HEAD, HEAD), jnp.float32))
    )
    after_pair = carried_in_2((shard_decay, first_pass[4]), "ctx", chain_link, identity)
    second_pass = mixer_pull((jnp.zeros((row_count, head_count, HEAD), jnp.float32), after_pair[1]))
    query_rec_grad = (first_pass[0] + second_pass[0]).reshape(row_count, local_width)
    key_rec_grad = (first_pass[1] + second_pass[1]).reshape(row_count, local_width)
    value_rec_grad = (first_pass[2] + second_pass[2]).reshape(row_count, local_width)
    log_rec_grad = (first_pass[3] + second_pass[3]).reshape(row_count, local_width)
    _, gate_pull = jax.vjp(gate_values, pre_query, pre_forget, forget_bias, bound_vec)
    query_pre_grad, forget_pre_grad, forget_bias_grad, bound_grad = gate_pull(
        (query_rec_grad, key_rec_grad, log_rec_grad)
    )
    _, table_pull = jax.vjp(lambda rows_in: lower_bound(rows_in, layer_index), bound_table)
    (table_grad,) = table_pull(bound_grad)
    proj_grad = jnp.concatenate(
        [query_pre_grad, forget_pre_grad, value_rec_grad, outgate_pre_grad], axis=1
    ).astype(jnp.bfloat16)
    first_part = contract_last(proj_grad, mix_full)
    mix_weight_grad = contract_first(first_low, proj_grad)
    first_total = lax.psum(first_part.astype(jnp.bfloat16), "tp").astype(jnp.float32)
    _, first_pull = jax.vjp(rms_norm, inputs, first_gain)
    input_part, first_gain_grad = first_pull(first_total)
    input_grad = resid_grad + input_part
    mix_summed, out_summed, ffn_summed, down_summed = (
        lax.psum_scatter(
            mix_weight_grad.astype(jnp.bfloat16), ("dp", "ctx"), scatter_dimension=0, tiled=True
        ).astype(jnp.float32),
        lax.psum_scatter(
            out_weight_grad.astype(jnp.bfloat16), ("dp", "ctx"), scatter_dimension=1, tiled=True
        ).astype(jnp.float32),
        lax.psum_scatter(
            ffn_weight_grad.astype(jnp.bfloat16), ("dp", "ctx"), scatter_dimension=0, tiled=True
        ).astype(jnp.float32),
        lax.psum_scatter(
            down_weight_grad.astype(jnp.bfloat16), ("dp", "ctx"), scatter_dimension=1, tiled=True
        ).astype(jnp.float32),
    )
    mix_shard, out_shard, ffn_shard, down_shard = (
        lax.all_gather(mix_summed.astype(jnp.bfloat16), "ctx", axis=0, tiled=True).astype(
            mix_summed.dtype
        ),
        lax.all_gather(out_summed.astype(jnp.bfloat16), "ctx", axis=1, tiled=True).astype(
            out_summed.dtype
        ),
        lax.all_gather(ffn_summed.astype(jnp.bfloat16), "ctx", axis=0, tiled=True).astype(
            ffn_summed.dtype
        ),
        lax.all_gather(down_summed.astype(jnp.bfloat16), "ctx", axis=1, tiled=True).astype(
            down_summed.dtype
        ),
    )
    first_sum, second_sum, group_sum, bias_sum, table_sum = (
        lax.psum(first_gain_grad.astype(jnp.bfloat16), ("dp", "ctx")).astype(jnp.float32),
        lax.psum(second_gain_grad.astype(jnp.bfloat16), ("dp", "ctx")).astype(jnp.float32),
        lax.psum(group_gain_grad.astype(jnp.bfloat16), ("dp", "ctx")).astype(jnp.float32),
        lax.psum(forget_bias_grad.astype(jnp.bfloat16), ("dp", "ctx")).astype(jnp.float32),
        lax.psum(table_grad.astype(jnp.bfloat16), ("dp", "ctx")).astype(jnp.float32),
    )
    return (
        block_out,
        input_grad,
        mix_shard[:, :local_width],
        mix_shard[:, local_width : 2 * local_width],
        mix_shard[:, 2 * local_width : 3 * local_width],
        mix_shard[:, 3 * local_width :],
        out_shard,
        ffn_shard[:, :hidden_width],
        ffn_shard[:, hidden_width:],
        down_shard,
        first_sum,
        second_sum,
        group_sum,
        bias_sum,
        table_sum,
    )


def solution(mesh):
    return jax.shard_map(
        body,
        mesh=mesh,
        in_specs=(
            P(("dp", "ctx"), None),
            P("dp", "tp"),
            P("dp", "tp"),
            P("dp", "tp"),
            P("dp", "tp"),
            P("tp", "dp"),
            P("dp", "tp"),
            P("dp", "tp"),
            P("tp", "dp"),
            P(),
            P(),
            P("tp"),
            P("tp"),
            P(None, "tp"),
            P(),
            P("dp"),
            P(("dp", "ctx"), None),
        ),
        out_specs=(
            P(("dp", "ctx"), None),
            P(("dp", "ctx"), None),
            P("dp", "tp"),
            P("dp", "tp"),
            P("dp", "tp"),
            P("dp", "tp"),
            P("tp", "dp"),
            P("dp", "tp"),
            P("dp", "tp"),
            P("tp", "dp"),
            P(),
            P(),
            P("tp"),
            P("tp"),
            P(None, "tp"),
        ),
        check_vma=False,
    )
```

profile of v0, /device:TPU:0, one launch (start us, length us, event | category | flops | bytes accessed | tf_op | source)
XLA Modules:
  0.0 2218.8 jit_solution(17821822070272523341)
XLA Ops:
  17.0 145.9 %all-gather.8.cloned.1.call-done = bf16[2048,2048]{1,0:T(8,128)(2,1)} async-done(((bf16[512,2048]{1,0:T(8,128)(2,1)}), bf16[2048,2048]{1,0:T(8,128)(2,1)}) %all-gather.8.cloned.1.call-update) | async-done | bytes 8388624 | tf_op jit(solution)/shard_map/all_gather | solution.py:170
  162.8 12.6 fusion.115
  209.9 13.7 fusion.85
  268.4 18.6 pad.557
  287.0 12.1 pad.558
  312.1 35.5 %pad.734 = f32[31,4,128,128]{2,3,1,0:T(8,128)} pad(f32[16,4,128,128]{2,3,1,0:T(8,128)} %pad_maximum_fusion.5, f32[]{:T(128)} %constant.113.clone.1), padding=0_0_1x0_0_0x0_0_0x0_0_0 | pad | bytes 12320772 | tf_op jit(solution)/shard_map/slice | solution.py:135
  347.6 35.6 %pad.559 = f32[32,4,128,128]{2,3,1,0:T(8,128)} pad(f32[16,4,128,128]{2,3,1,0:T(8,128)} %pad_maximum_fusion.5, f32[]{:T(128)} %constant.113.clone.1), padding=0_1_1x0_0_0x0_0_0x0_0_0 | pad | bytes 12582916 | tf_op jit(solution)/shard_map/pad | solution.py:128
  385.0 35.6 %pad.1005 = f32[32,4,128,128]{2,3,1,0:T(8,128)} pad(f32[16,4,128,128]{2,3,1,0:T(8,128)} %add.591, f32[]{:T(128)} %constant.113.clone.1), padding=1_0_1x0_0_0x0_0_0x0_0_0 | pad | bytes 12582916
  438.1 12.0 multiply_add_fusion
  450.2 16.1 fusion.19
  499.8 166.2 %all-reduce.122.cloned.1.call-done = f32[1024,2048]{1,0:T(8,128)} async-done(((f32[1024,2048]{1,0:T(8,128)}), f32[1024,2048]{1,0:T(8,128)}) %all-reduce.122.cloned.1.call-update) | async-done | bytes 8388624 | tf_op jit(solution)/shard_map/psum | solution.py:212
  675.0 194.9 %all-gather.12.cloned.1.call-done = bf16[2048,2816]{1,0:T(8,128)(2,1)} async-done(((bf16[512,2816]{1,0:T(8,128)(2,1)}), bf16[2048,2816]{1,0:T(8,128)(2,1)}) %all-gather.12.cloned.1.call-update) | async-done | bytes 11534352 | tf_op jit(solution)/shard_map/all_gather | solution.py:215
  869.9 20.0 fusion.177
  889.9 86.4 %all-gather.14.cloned.1.call-done = bf16[1408,2048]{1,0:T(8,128)(2,1)} async-done(((bf16[1408,512]{1,0:T(8,128)(2,1)}), bf16[1408,2048]{1,0:T(8,128)(2,1)}) %all-gather.14.cloned.1.call-update) | async-done | bytes 5767184 | tf_op jit(solution)/shard_map/all_gather | solution.py:216
  976.3 16.2 fusion.15
  995.1 16.8 fusion.20
  1012.0 10.5 convolution_convert_fusion.1
  1024.9 11.3 fusion.17
  1054.8 18.7 convolution_convert_fusion
  1073.5 11.1 convolution_convert_fusion.4
  1084.6 97.8 %all-reduce.124.cloned.1.call-done = f32[1024,2048]{1,0:T(8,128)} async-done(((f32[1024,2048]{1,0:T(8,128)}), f32[1024,2048]{1,0:T(8,128)}) %all-reduce.124.cloned.1.call-update) | async-done | bytes 8388624 | tf_op jit(solution)/shard_map/psum | solution.py:240
  1214.6 13.5 fusion.78
  1364.9 10.2 pad.622
  1401.0 12.0 pad.589
  1413.1 18.5 pad.623
  1435.8 18.6 pad.624
  1454.4 12.1 pad.590
  1466.5 16.7 pad.568
  1483.2 10.8 pad.602
  1494.0 15.5 multiply_reduce_fusion.5
  1510.5 35.6 %pad.625 = f32[32,4,128,128]{2,3,1,0:T(8,128)} pad(f32[16,4,128,128]{2,3,1,0:T(8,128)} %get-tuple-element.256, f32[]{:T(128)} %constant.113.clone.1), padding=1_0_1x0_0_0x0_0_0x0_0_0 | pad | bytes 12582916 | tf_op jit(solution)/shard_map/transpose(jvp())/pad | solution.py:128
  1546.0 35.5 %pad.591 = f32[32,4,128,128]{2,3,1,0:T(8,128)} pad(f32[16,4,128,128]{2,3,1,0:T(8,128)} %get-tuple-element.255, f32[]{:T(128)} %constant.113.clone.1), padding=1_0_1x0_0_0x0_0_0x0_0_0 | pad | bytes 12582916 | tf_op jit(solution)/shard_map/transpose(jvp())/pad | solution.py:128
  1590.3 35.6 %pad.592 = f32[32,4,128,128]{2,3,1,0:T(8,128)} pad(f32[16,4,128,128]{2,3,1,0:T(8,128)} %get-tuple-element.375, f32[]{:T(128)} %constant.113.clone.1), padding=0_1_1x0_0_0x0_0_0x0_0_0 | pad | bytes 12582916 | tf_op jit(solution)/shard_map/transpose(jvp())/pad | solution.py:128
  1625.9 35.7 %pad.626 = f32[32,4,128,128]{2,3,1,0:T(8,128)} pad(f32[16,4,128,128]{2,3,1,0:T(8,128)} %get-tuple-element.376, f32[]{:T(128)} %constant.113.clone.1), padding=0_1_1x0_0_0x0_0_0x0_0_0 | pad | bytes 12582916 | tf_op jit(solution)/shard_map/transpose(jvp())/pad | solution.py:128
  1661.7 33.6 %pad.562 = f32[32,4,128,128]{2,3,1,0:T(8,128)} pad(f32[15,4,128,128]{2,3,1,0:T(8,128)} %get-tuple-element.290, f32[]{:T(128)} %constant.113.clone.1), padding=2_1_1x0_0_0x0_0_0x0_0_0 | pad | bytes 12320772 | tf_op jit(solution)/shard_map/transpose(jvp())/pad | solution.py:128
  1695.3 33.7 %pad.597 = f32[32,4,128,128]{2,3,1,0:T(8,128)} pad(f32[15,4,128,128]{2,3,1,0:T(8,128)} %get-tuple-element.291, f32[]{:T(128)} %constant.113.clone.1), padding=2_1_1x0_0_0x0_0_0x0_0_0 | pad | bytes 12320772 | tf_op jit(solution)/shard_map/transpose(jvp())/pad | solution.py:128
  1729.0 10.8 fusion.18
  1752.8 10.0 add_add_fusion.3
  1771.4 15.1 fusion.83
  1786.5 9.8 add_add_fusion.2
  1810.3 19.3 fusion.176
  1830.9 11.6 fusion.41
  1842.6 13.5 fusion.81
  1877.1 12.9 convolution_convert_fusion.3
  1890.7 14.5 convolution_convert_fusion.2
  1913.4 152.0 %all-reduce.126.cloned.1.call-done = (bf16[1024,2048]{1,0:T(8,128)(2,1)}, bf16[1024,2048]{1,0:T(8,128)(2,1)}) async-done(((bf16[1024,2048]{1,0:T(8,128)(2,1)}, bf16[1024,2048]{1,0:T(8,128)(2,1)}), (bf16[1024,2048]{1,0:T(8,128)(2,1)}, bf16[1024,2048]{1,0:T(8,128)(2,1)})) %all-reduce.126.cloned.1.call-update) | async-done | bytes 8388624 | tf_op jit(solution)/shard_map/psum | solution.py:224
  2073.8 84.8 %reduce-scatter.5.cloned.1.call-done = bf16[256,2048]{1,0:T(8,128)(2,1)} async-done(((bf16[2048,2048]{1,0:T(8,128)(2,1)}), bf16[256,2048]{1,0:T(8,128)(2,1)}) %reduce-scatter.5.cloned.1.call-update) | async-done | bytes 1048592 | tf_op jit(solution)/shard_map/reduce_scatter | solution.py:287
  2164.6 26.3 %all-reduce.116 = (bf16[2048]{0:T(1024)(128)(2,1)S(1)}, bf16[2048]{0:T(1024)(128)(2,1)S(1)}, bf16[512]{0:T(512)(128)(2,1)S(1)}, bf16[512]{0:T(512)(128)(2,1)S(1)}, bf16[24,512]{1,0:T(8,128)(2,1)S(1)}) all-reduce(bf16[2048]{0:T(1024)(128)(2,1)S(1)} %get-tuple-element.200, ...), channel_id=1, replica_groups=mesh['dp'=4,'ctx'=2,'tp'=4] {'dp','ctx'}, use_global_device_ids=true, to_apply=%region_51.52 | all-reduce | flops 17408 | bytes 69632 | tf_op jit(solution)/shard_map/psum | solution.py:315
  (808 shorter events, 494.5 us)
Async XLA Ops:
  7.2 155.7 %all-gather.8.cloned.1.call-start = ((), (), s32[]{:S(2)}) async-start(), calls=%async_computation.4 | async-start | bytes 10485760 | tf_op jit(solution)/shard_map/all_gather | solution.py:170
  10.4 477.5 %all-gather.10.cloned.1.call-start = ((), (), s32[]{:S(2)}) async-start(), calls=%async_computation.5 | async-start | bytes 2621440 | tf_op jit(solution)/shard_map/all_gather | solution.py:171
  11.1 654.9 %all-reduce.122.cloned.1.call-start = ((), (), s32[]{:S(2)}) async-start(), calls=%async_computation.6 | async-start | bytes 16777216 | tf_op jit(solution)/shard_map/psum | solution.py:212
  12.7 150.1 %copy-start.194 = (f32[2048]{0:T(1024)S(1)}, f32[2048]{0:T(1024)}, u32[]{:S(2)}) copy-start(f32[2048]{0:T(1024)} %param.28) | copy-start | bytes 24580
  16.4 159.0 %copy-start.171 = (f32[1024]{0:T(1024)}, f32[1024]{0:T(1024)S(1)}, u32[]{:S(2)}) copy-start(f32[1024]{0:T(1024)S(1)} %fusion.149) | copy-start | bytes 12292
  16.6 158.8 %copy-start.178 = (f32[512]{0:T(512)}, f32[512]{0:T(512)S(1)}, u32[]{:S(2)}) copy-start(f32[512]{0:T(512)S(1)} %multiply_reduce_fusion.28) | copy-start | bytes 6148
  16.6 158.8 %copy-start.196 = (f32[512]{0:T(512)}, f32[512]{0:T(512)S(1)}, u32[]{:S(2)}) copy-start(f32[512]{0:T(512)S(1)} %broadcast_subtract_fusion) | copy-start | bytes 6148
  16.7 169.4 %copy-start.214 = (f32[32]{0:T(128)}, f32[32]{0:T(128)S(1)}, u32[]{:S(2)}) copy-start(f32[32]{0:T(128)S(1)} %get-tuple-element.269) | copy-start | bytes 388
  16.9 1024.1 %copy-start.73 = (pred[32,32,32]{2,1,0:T(8,128)(4,1)}, pred[32,32,32]{2,1,0:T(8,128)(4,1)S(1)}, u32[]{:S(2)}) copy-start(pred[32,32,32]{2,1,0:T(8,128)(4,1)S(1)} %compare_and_fusion) | copy-start | bytes 98308
  16.9 189.3 %copy-start.131 = (f32[32,32]{0,1:T(8,128)}, f32[32,32]{0,1:T(8,128)S(1)}, u32[]{:S(2)}) copy-start(f32[32,32]{0,1:T(8,128)S(1)} %get-tuple-element.440) | copy-start | bytes 12292
  16.9 415.8 %copy-start.129 = (f32[32,32]{0,1:T(8,128)}, f32[32,32]{0,1:T(8,128)S(1)}, u32[]{:S(2)}) copy-start(f32[32,32]{0,1:T(8,128)S(1)} %get-tuple-element.439) | copy-start | bytes 12292
  17.0 158.5 %copy-start.204 = (f32[512]{0:T(512)S(1)}, f32[512]{0:T(512)}, u32[]{:S(2)}) copy-start(f32[512]{0:T(512)} %param.31) | copy-start | bytes 6148
  184.2 22.0 copy-start
  187.5 36.2 %copy-start.125 = (f32[16,4,128]{2,1,0:T(4,128)}, f32[16,4,128]{2,1,0:T(4,128)S(1)}, u32[]{:S(2)}) copy-start(f32[16,4,128]{2,1,0:T(4,128)S(1)} %get-tuple-element.356) | copy-start | bytes 98308
  187.5 39.7 %copy-start.142 = (f32[8,4,128]{2,1,0:T(4,128)}, f32[8,4,128]{2,1,0:T(4,128)S(1)}, u32[]{:S(2)}) copy-start(f32[8,4,128]{2,1,0:T(4,128)S(1)} %get-tuple-element.380) | copy-start | bytes 49156
  187.6 42.5 %copy-start.155 = (f32[4,4,128]{2,1,0:T(4,128)}, f32[4,4,128]{2,1,0:T(4,128)S(1)}, u32[]{:S(2)}) copy-start(f32[4,4,128]{2,1,0:T(4,128)S(1)} %get-tuple-element.402) | copy-start | bytes 24580
  187.6 42.6 %copy-start.165 = (f32[2,4,128]{2,1,0:T(4,128)}, f32[2,4,128]{2,1,0:T(4,128)S(1)}, u32[]{:S(2)}) copy-start(f32[2,4,128]{2,1,0:T(4,128)S(1)} %get-tuple-element.421) | copy-start | bytes 12292
  187.7 42.6 %copy-start.198 = (f32[4,128]{1,0:T(4,128)}, f32[4,128]{1,0:T(4,128)S(1)}, u32[]{:S(2)}) copy-start(f32[4,128]{1,0:T(4,128)S(1)} %get-tuple-element.431) | copy-start | bytes 6148
  347.6 35.6 %copy-start.206 = (f32[1,4,128]{2,1,0:T(4,128)S(1)}, f32[1,4,128]{2,1,0:T(4,128)}, u32[]{:S(2)}) copy-start(f32[1,4,128]{2,1,0:T(4,128)} %get-tuple-element.266) | copy-start | bytes 6148
  424.2 600.7 %copy-start.88 = (f32[1,4,128,128]{2,3,1,0:T(8,128)}, f32[1,4,128,128]{2,3,1,0:T(8,128)S(1)}, u32[]{:S(2)}) copy-start(f32[1,4,128,128]{2,3,1,0:T(8,128)S(1)} %add_select_fusion) | copy-start | bytes 786436
  495.5 374.3 %all-gather.12.cloned.1.call-start = ((), (), s32[]{:S(2)}) async-start(), calls=%async_computation.7 | async-start | bytes 14417920 | tf_op jit(solution)/shard_map/all_gather | solution.py:215
  499.2 477.1 %all-gather.14.cloned.1.call-start = ((), (), s32[]{:S(2)}) async-start(), calls=%async_computation.8 | async-start | bytes 7208960 | tf_op jit(solution)/shard_map/all_gather | solution.py:216
  499.7 370.1 %copy-start.177 = (f32[2048]{0:T(1024)S(1)}, f32[2048]{0:T(1024)}, u32[]{:S(2)}) copy-start(f32[2048]{0:T(1024)} %param.29) | copy-start | bytes 24580
  499.8 682.7 %all-reduce.124.cloned.1.call-start = ((), (), s32[]{:S(2)}) async-start(), calls=%async_computation.9 | async-start | bytes 16777216 | tf_op jit(solution)/shard_map/psum | solution.py:240
  1011.9 865.1 %reduce-scatter.11.cloned.1.call-start = ((), (), s32[]{:S(2)}) async-start(), calls=%async_computation.15 | async-start | bytes 6488064 | tf_op jit(solution)/shard_map/reduce_scatter | solution.py:296
  1022.5 882.9 %reduce-scatter.9.cloned.1.call-start = ((), (), s32[]{:S(2)}) async-start(), calls=%async_computation.13 | async-start | bytes 12976128 | tf_op jit(solution)/shard_map/reduce_scatter | solution.py:293
  1073.5 833.1 %reduce-scatter.7.cloned.1.call-start = ((), (), s32[]{:S(2)}) async-start(), calls=%async_computation.12 | async-start | bytes 2359296 | tf_op jit(solution)/shard_map/reduce_scatter | solution.py:290
  1265.8 31.7 %copy-start.157 = (f32[8,4,128]{2,1,0:T(4,128)}, f32[8,4,128]{2,1,0:T(4,128)S(1)}, u32[]{:S(2)}) copy-start(f32[8,4,128]{2,1,0:T(4,128)S(1)} %slice.479) | copy-start | bytes 49156
  1265.9 31.7 %copy-start.158 = (f32[8,4,128]{2,1,0:T(4,128)}, f32[8,4,128]{2,1,0:T(4,128)S(1)}, u32[]{:S(2)}) copy-start(f32[8,4,128]{2,1,0:T(4,128)S(1)} %slice.471) | copy-start | bytes 49156
  1546.0 35.5 %copy-start.126 = (f32[16,4,128]{2,1,0:T(4,128)S(1)}, f32[16,4,128]{2,1,0:T(4,128)}, u32[]{:S(2)}) copy-start(f32[16,4,128]{2,1,0:T(4,128)} %copy-done.125) | copy-start | bytes 98308
  1695.3 33.7 %copy-start.24 = (f32[32,4,128,32]{2,3,1,0:T(8,128)S(1)}, f32[32,4,128,32]{2,3,1,0:T(8,128)}, u32[]{:S(2)}) copy-start(f32[32,4,128,32]{2,3,1,0:T(8,128)} %copy-done.23) | copy-start | bytes 6291460
  1695.3 33.7 %copy-start.89 = (f32[1,4,128,128]{2,3,1,0:T(8,128)S(1)}, f32[1,4,128,128]{2,3,1,0:T(8,128)}, u32[]{:S(2)}) copy-start(f32[1,4,128,128]{2,3,1,0:T(8,128)} %copy-done.88) | copy-start | bytes 786436
  1771.4 33.5 %slice-start.1 = ((s8[8388608]{0:T(1024)(128)(4,1)}), s8[4194304]{0:T(1024)(128)(4,1)S(1)}, s32[]{:S(2)}) async-start(s8[8388608]{0:T(1024)(128)(4,1)} %bitcast.242), calls=%async_computation.19 | async-start | bytes 8388608
  1808.7 20.9 copy-start.134
  1808.7 20.9 copy-start.135
  1808.7 20.9 slice-start.17
  1808.7 20.9 slice-start.18
  1808.8 20.9 copy-start.215
  1808.8 101.3 %all-gather.20.cloned.1.call-start = ((), (), s32[]{:S(2)}) async-start(), calls=%async_computation.16 | async-start | bytes 2162688 | tf_op jit(solution)/shard_map/all_gather | solution.py:310
  1810.3 20.6 copy-start.48
  1810.3 20.6 copy-start.49
  1810.3 20.6 copy-start.54
  1810.3 20.6 copy-start.55
  1877.1 188.4 %all-reduce.126.cloned.1.call-start = ((), (), s32[]{:S(2)}) async-start(), calls=%async_computation.17 | async-start | bytes 16777216 | tf_op jit(solution)/shard_map/psum | solution.py:224
  1890.0 268.6 %reduce-scatter.5.cloned.1.call-start = ((), (), s32[]{:S(2)}) async-start(), calls=%async_computation.10 | async-start | bytes 9437184 | tf_op jit(solution)/shard_map/reduce_scatter | solution.py:287
  1905.3 298.1 %all-gather.18.cloned.1.call-start = ((), (), s32[]{:S(2)}) async-start(), calls=%async_computation.14 | async-start | bytes 4325376 | tf_op jit(solution)/shard_map/all_gather | solution.py:307
  1906.0 302.0 %all-gather.16.cloned.1.call-start = ((), (), s32[]{:S(2)}) async-start(), calls=%async_computation.11 | async-start | bytes 3145728 | tf_op jit(solution)/shard_map/all_gather | solution.py:301
  2158.6 35.2 %copy-start.168 = (f32[1024]{0:T(1024)S(1)}, f32[1024]{0:T(1024)}, u32[]{:S(2)}) copy-start(f32[1024]{0:T(1024)} %copy-done.167) | copy-start | bytes 12292
  (213 other events, 1256.3 us)
Sparse Core Ops, SparseCore 0:
  10.5 152.3 all-gather.7
  164.4 44.1 all-gather.9
  495.6 170.3 all-reduce.121
  668.1 201.7 all-gather.11
  871.3 104.8 all-gather.13
  1012.0 170.3 all-reduce.123
  1184.7 65.5 reduce-scatter.10
  1252.6 117.6 reduce-scatter.8
  1808.8 36.2 reduce-scatter.6
  1877.2 10.0 all-gather.19
  1891.6 173.7 all-reduce.125
  2068.3 90.2 reduce-scatter.4
  2160.2 10.1 all-gather.17
  2171.8 11.7 all-gather.15
where the time goes:
time: 2250 us; the launch traced here: 2220 us
  waiting for transfers between devices  930 us (41%)
  local copies, waits for them, and re-layouts  640 us (28%)
  matrix products  319 us (14%)
  other arithmetic  275 us (12%)
  blocking collectives  36.4 us (2%)
    pad x74, local copies, waits for them, and re-layouts, block_parts(): lax.associative_scan(chain_link, (carried, states), axis=0)  483 us
    all_gather x1, waiting for transfers between devices, body(): lax.all_gather(ffn_local, 'dp', axis=0, tiled=True)  195 us
    psum x1, waiting for transfers between devices, body(): resid = inputs + lax.psum(mix_partial, 'tp')  166 us
    psum x1, waiting for transfers between devices, body(): lax.psum(ffn_partial.astype(jnp.bfloat16), 'tp').astype(jnp.float32)  152 us
    all_gather x1, waiting for transfers between devices, body(): lax.all_gather(mix_local, 'dp', axis=0, tiled=True)  146 us
    psum x1, waiting for transfers between devices, body(): second_total = lax.psum(second_part, 'tp')  97.8 us
    all_gather x1, waiting for transfers between devices, body(): lax.all_gather(ffn_down, 'dp', axis=1, tiled=True)  86.4 us
    reduce_scatter x1, waiting for transfers between devices, body(): lax.psum_scatter(mix_weight_grad.astype(jnp.bfloat16), ('dp', 'ctx'), sca...  84.8 us
  transfers between devices with their start and end apart: 14, of which 7 were waited for; matrix products, arithmetic and copies ran while one was open for 51% of the time, Pallas kernels for 0%

commit v1 on v0

--- a/solution.py
+++ b/solution.py
@@ -8,6 +8,18 @@
 HIGH = lax.Precision.HIGHEST
 EPS_NORM = 1e-06
 EPS_GROUP = 1e-05
+
+
+def ring_gather(array, axis, dim):
+    ways, here, hop = (lax.axis_size(axis), lax.axis_index(axis), array.shape[dim])
+    dims = [n * ways if d == dim else n for d, n in enumerate(array.shape)]
+    full = lax.dynamic_update_slice_in_dim(
+        jnp.zeros(dims, array.dtype), array, here * hop, axis=dim
+    )
+    for far in range(1, ways):
+        array = lax.ppermute(array, axis, [(d, (d + 1) % ways) for d in range(ways)])
+        full = lax.dynamic_update_slice_in_dim(full, array, (here - far) % ways * hop, axis=dim)
+    return full
 
 
 def carried_in(value, axis, join, neutral):
@@ -212,7 +224,7 @@
     resid = inputs + lax.psum(mix_partial, "tp")
     second_low = rms_norm(resid, second_gain).astype(jnp.bfloat16)
     ffn_full, down_full = (
-        lax.all_gather(ffn_local, "dp", axis=0, tiled=True),
+        ring_gather(ffn_local, "dp", 0),
         lax.all_gather(ffn_down, "dp", axis=1, tiled=True),
     )
     gate_up = jnp.dot(second_low, ffn_full, preferred_element_type=jnp.float32)

time: 2250 us -> 2250 us (level)
  local copies, waits for them, and re-layouts: 640 us -> 665 us
    ppermute x0 -> x3, waiting for transfers between devices: none -> 200 us  [ring_gather(): lax.ppermute(array, axis, [(d, (d + 1) % ways) for d in range(ways)])]
    psum x1, waiting for transfers between devices: 166 us -> 0.01 us  [body(): resid = inputs + lax.psum(mix_partial, 'tp')]
    all_gather x1, waiting for transfers between devices: 86.4 us -> 44.6 us  [body(): lax.all_gather(ffn_down, 'dp', axis=1, tiled=True)]
    unnamed x468 -> x469, local copies, waits for them, and re-layouts: 79.2 us -> 82.4 us
  transfers between devices with their start and end apart: 14 -> 17, of which waited for: 7 -> 9; matrix products, arithmetic and copies ran while one was open for 51% -> 53% of each run, Pallas kernels for 0% -> 0%
where the time goes in v1:
time: 2250 us; the launch traced here: 2220 us
  waiting for transfers between devices  911 us (40%)
  local copies, waits for them, and re-layouts  665 us (30%)
  matrix products  319 us (14%)
  other arithmetic  267 us (12%)
  blocking collectives  36.4 us (2%)
    pad x74, local copies, waits for them, and re-layouts, block_parts(): lax.associative_scan(chain_link, (carried, states), axis=0)  484 us
    ppermute x3, waiting for transfers between devices, ring_gather(): lax.ppermute(array, axis, [(d, (d + 1) % ways) for d in range(ways)])  200 us
    all_gather x1, waiting for transfers between devices, body(): lax.all_gather(ffn_local, 'dp', axis=0, tiled=True)  184 us
    psum x1, waiting for transfers between devices, body(): lax.psum(ffn_partial.astype(jnp.bfloat16), 'tp').astype(jnp.float32)  152 us
    all_gather x1, waiting for transfers between devices, body(): lax.all_gather(mix_local, 'dp', axis=0, tiled=True)  146 us
    psum x1, waiting for transfers between devices, body(): second_total = lax.psum(second_part, 'tp')  97.7 us
    reduce_scatter x1, waiting for transfers between devices, body(): lax.psum_scatter(mix_weight_grad.astype(jnp.bfloat16), ('dp', 'ctx'), sca...  84.9 us
    unnamed x469, local copies, waits for them, and re-layouts  82.4 us
  transfers between devices with their start and end apart: 17, of which 9 were waited for; matrix products, arithmetic and copies ran while one was open for 53% of the time, Pallas kernels for 0%

profile of v1, /device:TPU:0, one launch (start us, length us, event | category | flops | bytes accessed | tf_op | source)
XLA Modules:
  0.0 2218.3 jit_solution(7412519946979133656)
XLA Ops:
  17.0 145.9 %all-gather.8.cloned.1.call-done = bf16[2048,2048]{1,0:T(8,128)(2,1)} async-done(((bf16[512,2048]{1,0:T(8,128)(2,1)}), bf16[2048,2048]{1,0:T(8,128)(2,1)}) %all-gather.8.cloned.1.call-update) | async-done | bytes 8388624 | tf_op jit(solution)/shard_map/all_gather | solution.py:182
  162.8 12.6 fusion.115
  209.9 13.7 fusion.85
  268.4 18.7 pad.557
  287.1 12.1 pad.558
  312.0 35.6 %pad.732 = f32[31,4,128,128]{2,3,1,0:T(8,128)} pad(f32[16,4,128,128]{2,3,1,0:T(8,128)} %pad_maximum_fusion.5, f32[]{:T(128)} %constant.142.clone.1), padding=0_0_1x0_0_0x0_0_0x0_0_0 | pad | bytes 12320772 | tf_op jit(solution)/shard_map/slice | solution.py:147
  347.6 35.4 %pad.559 = f32[32,4,128,128]{2,3,1,0:T(8,128)} pad(f32[16,4,128,128]{2,3,1,0:T(8,128)} %pad_maximum_fusion.5, f32[]{:T(128)} %constant.142.clone.1), padding=0_1_1x0_0_0x0_0_0x0_0_0 | pad | bytes 12582916 | tf_op jit(solution)/shard_map/pad | solution.py:140
  384.8 35.5 %pad.1001 = f32[32,4,128,128]{2,3,1,0:T(8,128)} pad(f32[16,4,128,128]{2,3,1,0:T(8,128)} %add.616, f32[]{:T(128)} %constant.142.clone.1), padding=1_0_1x0_0_0x0_0_0x0_0_0 | pad | bytes 12582916
  437.8 11.6 multiply_add_fusion
  449.5 16.1 fusion.19
  499.3 66.6 %collective-permute-done = bf16[512,2816]{1,0:T(8,128)(2,1)} collective-permute-done((bf16[512,2816]{1,0:T(8,128)(2,1)}, bf16[512,2816]{1,0:T(8,128)(2,1)}, u32[]{:S(2)}, u32[]{:S(2)}) %collective-permute-start) | collective-permute-done | bytes 2883616 | tf_op jit(solution)/shard_map/ppermute | solution.py:20
  565.9 65.9 %collective-permute-done.1 = bf16[512,2816]{1,0:T(8,128)(2,1)} collective-permute-done((bf16[512,2816]{1,0:T(8,128)(2,1)}, bf16[512,2816]{1,0:T(8,128)(2,1)}, u32[]{:S(2)}, u32[]{:S(2)}) %collective-permute-start.1) | collective-permute-done | bytes 2883616 | tf_op jit(solution)/shard_map/ppermute | solution.py:20
  648.1 67.1 %collective-permute-done.2 = bf16[512,2816]{1,0:T(8,128)(2,1)} collective-permute-done((bf16[512,2816]{1,0:T(8,128)(2,1)}, bf16[512,2816]{1,0:T(8,128)(2,1)}, u32[]{:S(2)}, u32[]{:S(2)}) %collective-permute-start.2) | collective-permute-done | bytes 2883616 | tf_op jit(solution)/shard_map/ppermute | solution.py:20
  727.9 17.6 fusion.177
  745.5 44.6 %all-gather.12.cloned.1.call-done = bf16[1408,2048]{1,0:T(8,128)(2,1)} async-done(((bf16[1408,512]{1,0:T(8,128)(2,1)}), bf16[1408,2048]{1,0:T(8,128)(2,1)}) %all-gather.12.cloned.1.call-update) | async-done | bytes 5767184 | tf_op jit(solution)/shard_map/all_gather | solution.py:228
  790.1 17.2 fusion.15
  807.3 184.2 %all-gather.14.cloned.1.call-done = bf16[2048,2816]{1,0:T(8,128)(2,1)} async-done(((bf16[512,2816]{1,0:T(8,128)(2,1)}), bf16[2048,2816]{1,0:T(8,128)(2,1)}) %all-gather.14.cloned.1.call-update) | async-done | bytes 11534352 | tf_op jit(solution)/shard_map/all_gather | solution.py:241
  991.5 18.7 fusion.20
  1010.3 10.5 convolution_convert_fusion.1
  1023.2 11.3 fusion.17
  1053.2 18.6 convolution_convert_fusion
  1071.8 11.1 convolution_convert_fusion.4
  1082.9 97.7 %all-reduce.124.cloned.1.call-done = f32[1024,2048]{1,0:T(8,128)} async-done(((f32[1024,2048]{1,0:T(8,128)}), f32[1024,2048]{1,0:T(8,128)}) %all-reduce.124.cloned.1.call-update) | async-done | bytes 8388624 | tf_op jit(solution)/shard_map/psum | solution.py:252
  1212.8 13.5 fusion.78
  1363.3 10.1 pad.622
  1399.4 12.1 pad.589
  1411.5 18.5 pad.623
  1434.2 18.7 pad.624
  1452.9 12.1 pad.590
  1465.0 16.8 pad.568
  1481.8 10.9 pad.602
  1492.7 15.5 multiply_reduce_fusion.5
  1509.2 35.6 %pad.625 = f32[32,4,128,128]{2,3,1,0:T(8,128)} pad(f32[16,4,128,128]{2,3,1,0:T(8,128)} %get-tuple-element.256, f32[]{:T(128)} %constant.142.clone.1), padding=1_0_1x0_0_0x0_0_0x0_0_0 | pad | bytes 12582916 | tf_op jit(solution)/shard_map/transpose(jvp())/pad | solution.py:140
  1544.8 35.8 %pad.591 = f32[32,4,128,128]{2,3,1,0:T(8,128)} pad(f32[16,4,128,128]{2,3,1,0:T(8,128)} %get-tuple-element.255, f32[]{:T(128)} %constant.142.clone.1), padding=1_0_1x0_0_0x0_0_0x0_0_0 | pad | bytes 12582916 | tf_op jit(solution)/shard_map/transpose(jvp())/pad | solution.py:140
  1589.4 35.7 %pad.592 = f32[32,4,128,128]{2,3,1,0:T(8,128)} pad(f32[16,4,128,128]{2,3,1,0:T(8,128)} %get-tuple-element.375, f32[]{:T(128)} %constant.142.clone.1), padding=0_1_1x0_0_0x0_0_0x0_0_0 | pad | bytes 12582916 | tf_op jit(solution)/shard_map/transpose(jvp())/pad | solution.py:140
  1625.1 35.7 %pad.626 = f32[32,4,128,128]{2,3,1,0:T(8,128)} pad(f32[16,4,128,128]{2,3,1,0:T(8,128)} %get-tuple-element.376, f32[]{:T(128)} %constant.142.clone.1), padding=0_1_1x0_0_0x0_0_0x0_0_0 | pad | bytes 12582916 | tf_op jit(solution)/shard_map/transpose(jvp())/pad | solution.py:140
  1660.9 33.6 %pad.562 = f32[32,4,128,128]{2,3,1,0:T(8,128)} pad(f32[15,4,128,128]{2,3,1,0:T(8,128)} %get-tuple-element.290, f32[]{:T(128)} %constant.142.clone.1), padding=2_1_1x0_0_0x0_0_0x0_0_0 | pad | bytes 12320772 | tf_op jit(solution)/shard_map/transpose(jvp())/pad | solution.py:140
  1694.5 33.8 %pad.597 = f32[32,4,128,128]{2,3,1,0:T(8,128)} pad(f32[15,4,128,128]{2,3,1,0:T(8,128)} %get-tuple-element.291, f32[]{:T(128)} %constant.142.clone.1), padding=2_1_1x0_0_0x0_0_0x0_0_0 | pad | bytes 12320772 | tf_op jit(solution)/shard_map/transpose(jvp())/pad | solution.py:140
  1728.3 10.8 fusion.18
  1770.7 15.0 fusion.83
  1809.7 19.4 fusion.176
  1830.4 11.6 fusion.41
  1842.1 13.5 fusion.81
  1876.6 12.9 convolution_convert_fusion.3
  1890.1 14.5 convolution_convert_fusion.2
  1912.8 152.1 %all-reduce.126.cloned.1.call-done = (bf16[1024,2048]{1,0:T(8,128)(2,1)}, bf16[1024,2048]{1,0:T(8,128)(2,1)}) async-done(((bf16[1024,2048]{1,0:T(8,128)(2,1)}, bf16[1024,2048]{1,0:T(8,128)(2,1)}), (bf16[1024,2048]{1,0:T(8,128)(2,1)}, bf16[1024,2048]{1,0:T(8,128)(2,1)})) %all-reduce.126.cloned.1.call-update) | async-done | bytes 8388624 | tf_op jit(solution)/shard_map/psum | solution.py:236
  2073.2 84.9 %reduce-scatter.5.cloned.1.call-done = bf16[256,2048]{1,0:T(8,128)(2,1)} async-done(((bf16[2048,2048]{1,0:T(8,128)(2,1)}), bf16[256,2048]{1,0:T(8,128)(2,1)}) %reduce-scatter.5.cloned.1.call-update) | async-done | bytes 1048592 | tf_op jit(solution)/shard_map/reduce_scatter | solution.py:299
  2164.1 26.3 %all-reduce.116 = (bf16[2048]{0:T(1024)(128)(2,1)S(1)}, bf16[2048]{0:T(1024)(128)(2,1)S(1)}, bf16[512]{0:T(512)(128)(2,1)S(1)}, bf16[512]{0:T(512)(128)(2,1)S(1)}, bf16[24,512]{1,0:T(8,128)(2,1)S(1)}) all-reduce(bf16[2048]{0:T(1024)(128)(2,1)S(1)} %get-tuple-element.200, ...), channel_id=1, replica_groups=mesh['dp'=4,'ctx'=2,'tp'=4] {'dp','ctx'}, use_global_device_ids=true, to_apply=%region_51.52 | all-reduce | flops 17408 | bytes 69632 | tf_op jit(solution)/shard_map/psum | solution.py:327
  (820 shorter events, 531.9 us)
Async XLA Ops:
  7.2 155.7 %all-gather.8.cloned.1.call-start = ((), (), s32[]{:S(2)}) async-start(), calls=%async_computation.4 | async-start | bytes 10485760 | tf_op jit(solution)/shard_map/all_gather | solution.py:182
  10.4 476.8 %all-gather.10.cloned.1.call-start = ((), (), s32[]{:S(2)}) async-start(), calls=%async_computation.5 | async-start | bytes 2621440 | tf_op jit(solution)/shard_map/all_gather | solution.py:183
  11.1 707.8 %all-reduce.122.cloned.1.call-start = ((), (), s32[]{:S(2)}) async-start(), calls=%async_computation.6 | async-start | bytes 16777216 | tf_op jit(solution)/shard_map/psum | solution.py:224
  12.7 150.1 %copy-start.196 = (f32[2048]{0:T(1024)S(1)}, f32[2048]{0:T(1024)}, u32[]{:S(2)}) copy-start(f32[2048]{0:T(1024)} %param.28) | copy-start | bytes 24580
  16.4 159.0 %copy-start.173 = (f32[1024]{0:T(1024)}, f32[1024]{0:T(1024)S(1)}, u32[]{:S(2)}) copy-start(f32[1024]{0:T(1024)S(1)} %fusion.149) | copy-start | bytes 12292
  16.6 158.8 %copy-start.180 = (f32[512]{0:T(512)}, f32[512]{0:T(512)S(1)}, u32[]{:S(2)}) copy-start(f32[512]{0:T(512)S(1)} %multiply_reduce_fusion.28) | copy-start | bytes 6148
  16.6 158.8 %copy-start.198 = (f32[512]{0:T(512)}, f32[512]{0:T(512)S(1)}, u32[]{:S(2)}) copy-start(f32[512]{0:T(512)S(1)} %broadcast_subtract_fusion) | copy-start | bytes 6148
  16.7 169.3 %copy-start.216 = (f32[32]{0:T(128)}, f32[32]{0:T(128)S(1)}, u32[]{:S(2)}) copy-start(f32[32]{0:T(128)S(1)} %get-tuple-element.269) | copy-start | bytes 388
  16.9 1022.5 %copy-start.74 = (pred[32,32,32]{2,1,0:T(8,128)(4,1)}, pred[32,32,32]{2,1,0:T(8,128)(4,1)S(1)}, u32[]{:S(2)}) copy-start(pred[32,32,32]{2,1,0:T(8,128)(4,1)S(1)} %compare_and_fusion) | copy-start | bytes 98308
  16.9 189.2 %copy-start.133 = (f32[32,32]{0,1:T(8,128)}, f32[32,32]{0,1:T(8,128)S(1)}, u32[]{:S(2)}) copy-start(f32[32,32]{0,1:T(8,128)S(1)} %get-tuple-element.440) | copy-start | bytes 12292
  16.9 415.5 %copy-start.131 = (f32[32,32]{0,1:T(8,128)}, f32[32,32]{0,1:T(8,128)S(1)}, u32[]{:S(2)}) copy-start(f32[32,32]{0,1:T(8,128)S(1)} %get-tuple-element.439) | copy-start | bytes 12292
  17.0 158.5 %copy-start.206 = (f32[512]{0:T(512)S(1)}, f32[512]{0:T(512)}, u32[]{:S(2)}) copy-start(f32[512]{0:T(512)} %param.31) | copy-start | bytes 6148
  184.1 22.0 copy-start.1
  187.5 36.2 %copy-start.127 = (f32[16,4,128]{2,1,0:T(4,128)}, f32[16,4,128]{2,1,0:T(4,128)S(1)}, u32[]{:S(2)}) copy-start(f32[16,4,128]{2,1,0:T(4,128)S(1)} %get-tuple-element.356) | copy-start | bytes 98308
  187.5 39.7 %copy-start.144 = (f32[8,4,128]{2,1,0:T(4,128)}, f32[8,4,128]{2,1,0:T(4,128)S(1)}, u32[]{:S(2)}) copy-start(f32[8,4,128]{2,1,0:T(4,128)S(1)} %get-tuple-element.380) | copy-start | bytes 49156
  187.6 42.4 %copy-start.157 = (f32[4,4,128]{2,1,0:T(4,128)}, f32[4,4,128]{2,1,0:T(4,128)S(1)}, u32[]{:S(2)}) copy-start(f32[4,4,128]{2,1,0:T(4,128)S(1)} %get-tuple-element.402) | copy-start | bytes 24580
  187.6 42.5 %copy-start.167 = (f32[2,4,128]{2,1,0:T(4,128)}, f32[2,4,128]{2,1,0:T(4,128)S(1)}, u32[]{:S(2)}) copy-start(f32[2,4,128]{2,1,0:T(4,128)S(1)} %get-tuple-element.421) | copy-start | bytes 12292
  187.6 42.5 %copy-start.200 = (f32[4,128]{1,0:T(4,128)}, f32[4,128]{1,0:T(4,128)S(1)}, u32[]{:S(2)}) copy-start(f32[4,128]{1,0:T(4,128)S(1)} %get-tuple-element.431) | copy-start | bytes 6148
  347.6 35.5 %copy-start.208 = (f32[1,4,128]{2,1,0:T(4,128)S(1)}, f32[1,4,128]{2,1,0:T(4,128)}, u32[]{:S(2)}) copy-start(f32[1,4,128]{2,1,0:T(4,128)} %get-tuple-element.266) | copy-start | bytes 6148
  423.9 599.3 %copy-start.89 = (f32[1,4,128,128]{2,3,1,0:T(8,128)}, f32[1,4,128,128]{2,3,1,0:T(8,128)S(1)}, u32[]{:S(2)}) copy-start(f32[1,4,128,128]{2,3,1,0:T(8,128)S(1)} %add_select_fusion) | copy-start | bytes 786436
  494.7 295.4 %all-gather.12.cloned.1.call-start = ((), (), s32[]{:S(2)}) async-start(), calls=%async_computation.7 | async-start | bytes 7208960 | tf_op jit(solution)/shard_map/all_gather | solution.py:228
  495.3 496.3 %all-gather.14.cloned.1.call-start = ((), (), s32[]{:S(2)}) async-start(), calls=%async_computation.8 | async-start | bytes 14417920 | tf_op jit(solution)/shard_map/all_gather | solution.py:241
  499.2 66.7 %collective-permute-start = (bf16[512,2816]{1,0:T(8,128)(2,1)}, bf16[512,2816]{1,0:T(8,128)(2,1)}, u32[]{:S(2)}, u32[]{:S(2)}) collective-permute-start(bf16[512,2816]{1,0:T(8,128)(2,1)} %constant_dynamic-update-slice_fusion), channel_id=1, source_target_pairs={{0,8},{8,16},{16,24},{24,0},{1,9},{9,17},{17,25},{25,1},{2,10},{10... | collective-permute-start | bytes 8650760 | tf_op jit(solution)/shard_map/ppermute | solution.py:20
  499.2 681.4 %all-reduce.124.cloned.1.call-start = ((), (), s32[]{:S(2)}) async-start(), calls=%async_computation.9 | async-start | bytes 16777216 | tf_op jit(solution)/shard_map/psum | solution.py:252
  565.9 65.9 %collective-permute-start.1 = (bf16[512,2816]{1,0:T(8,128)(2,1)}, bf16[512,2816]{1,0:T(8,128)(2,1)}, u32[]{:S(2)}, u32[]{:S(2)}) collective-permute-start(bf16[512,2816]{1,0:T(8,128)(2,1)} %collective-permute-done), channel_id=1, source_target_pairs={{0,8},{8,16},{16,24},{24,0},{1,9},{9,17},{17,25},{25,1},{2,10},{10... | collective-permute-start | bytes 8650760 | tf_op jit(solution)/shard_map/ppermute | solution.py:20
  631.8 83.5 %collective-permute-start.2 = (bf16[512,2816]{1,0:T(8,128)(2,1)}, bf16[512,2816]{1,0:T(8,128)(2,1)}, u32[]{:S(2)}, u32[]{:S(2)}) collective-permute-start(bf16[512,2816]{1,0:T(8,128)(2,1)} %collective-permute-done.1), channel_id=1, source_target_pairs={{0,8},{8,16},{16,24},{24,0},{1,9},{9,17},{17,25},{25,1},{2,10},{10... | collective-permute-start | bytes 8650760 | tf_op jit(solution)/shard_map/ppermute | solution.py:20
  1010.2 866.2 %reduce-scatter.11.cloned.1.call-start = ((), (), s32[]{:S(2)}) async-start(), calls=%async_computation.15 | async-start | bytes 6488064 | tf_op jit(solution)/shard_map/reduce_scatter | solution.py:308
  1020.8 884.0 %reduce-scatter.9.cloned.1.call-start = ((), (), s32[]{:S(2)}) async-start(), calls=%async_computation.13 | async-start | bytes 12976128 | tf_op jit(solution)/shard_map/reduce_scatter | solution.py:305
  1071.8 834.2 %reduce-scatter.7.cloned.1.call-start = ((), (), s32[]{:S(2)}) async-start(), calls=%async_computation.12 | async-start | bytes 2359296 | tf_op jit(solution)/shard_map/reduce_scatter | solution.py:302
  1264.2 31.7 %copy-start.159 = (f32[8,4,128]{2,1,0:T(4,128)}, f32[8,4,128]{2,1,0:T(4,128)S(1)}, u32[]{:S(2)}) copy-start(f32[8,4,128]{2,1,0:T(4,128)S(1)} %slice.479) | copy-start | bytes 49156
  1264.2 31.6 %copy-start.160 = (f32[8,4,128]{2,1,0:T(4,128)}, f32[8,4,128]{2,1,0:T(4,128)S(1)}, u32[]{:S(2)}) copy-start(f32[8,4,128]{2,1,0:T(4,128)S(1)} %slice.471) | copy-start | bytes 49156
  1544.8 35.8 %copy-start.128 = (f32[16,4,128]{2,1,0:T(4,128)S(1)}, f32[16,4,128]{2,1,0:T(4,128)}, u32[]{:S(2)}) copy-start(f32[16,4,128]{2,1,0:T(4,128)} %copy-done.127) | copy-start | bytes 98308
  1694.5 33.8 %copy-start.25 = (f32[32,4,128,32]{2,3,1,0:T(8,128)S(1)}, f32[32,4,128,32]{2,3,1,0:T(8,128)}, u32[]{:S(2)}) copy-start(f32[32,4,128,32]{2,3,1,0:T(8,128)} %copy-done.24) | copy-start | bytes 6291460
  1694.5 33.8 %copy-start.90 = (f32[1,4,128,128]{2,3,1,0:T(8,128)S(1)}, f32[1,4,128,128]{2,3,1,0:T(8,128)}, u32[]{:S(2)}) copy-start(f32[1,4,128,128]{2,3,1,0:T(8,128)} %copy-done.89) | copy-start | bytes 786436
  1770.7 33.4 %slice-start.1 = ((s8[8388608]{0:T(1024)(128)(4,1)}), s8[4194304]{0:T(1024)(128)(4,1)S(1)}, s32[]{:S(2)}) async-start(s8[8388608]{0:T(1024)(128)(4,1)} %bitcast.242), calls=%async_computation.19 | async-start | bytes 8388608
  1808.0 21.1 copy-start.136
  1808.0 21.1 copy-start.137
  1808.0 21.1 slice-start.17
  1808.1 21.1 slice-start.18
  1808.1 21.1 copy-start.217
  1808.1 101.4 %all-gather.20.cloned.1.call-start = ((), (), s32[]{:S(2)}) async-start(), calls=%async_computation.16 | async-start | bytes 2162688 | tf_op jit(solution)/shard_map/all_gather | solution.py:322
  1809.6 20.7 copy-start.49
  1809.6 20.7 copy-start.50
  1876.5 188.4 %all-reduce.126.cloned.1.call-start = ((), (), s32[]{:S(2)}) async-start(), calls=%async_computation.17 | async-start | bytes 16777216 | tf_op jit(solution)/shard_map/psum | solution.py:236
  1889.5 268.6 %reduce-scatter.5.cloned.1.call-start = ((), (), s32[]{:S(2)}) async-start(), calls=%async_computation.10 | async-start | bytes 9437184 | tf_op jit(solution)/shard_map/reduce_scatter | solution.py:299
  1904.7 298.2 %all-gather.18.cloned.1.call-start = ((), (), s32[]{:S(2)}) async-start(), calls=%async_computation.14 | async-start | bytes 4325376 | tf_op jit(solution)/shard_map/all_gather | solution.py:319
  1905.5 302.1 %all-gather.16.cloned.1.call-start = ((), (), s32[]{:S(2)}) async-start(), calls=%async_computation.11 | async-start | bytes 3145728 | tf_op jit(solution)/shard_map/all_gather | solution.py:313
  2158.1 35.2 %copy-start.170 = (f32[1024]{0:T(1024)S(1)}, f32[1024]{0:T(1024)}, u32[]{:S(2)}) copy-start(f32[1024]{0:T(1024)} %copy-done.169) | copy-start | bytes 12292
  (216 other events, 1309.9 us)
Sparse Core Ops, SparseCore 0:
  10.5 152.3 all-gather.7
  164.4 44.1 all-gather.9
  494.8 170.3 all-reduce.121
  666.7 123.4 all-gather.11
  792.2 199.2 all-gather.13
  1010.4 170.2 all-reduce.123
  1183.0 65.5 reduce-scatter.10
  1250.9 117.6 reduce-scatter.8
  1808.1 36.3 reduce-scatter.6
  1876.6 10.0 all-gather.19
  1891.1 173.7 all-reduce.125
  2067.8 90.2 reduce-scatter.4
  2159.7 10.1 all-gather.17
  2171.3 11.7 all-gather.15
